TPU v7x, 32 devices: a whole 2x2x4 slice. The times are simulated.
32 devices in a mesh: row: 2 (over x), col: 16 (over z, y, core).
Axes of the slice: x: 2, y: 2, z: 4, core: 2. Of those that a mesh axis runs over, the one named last changes fastest.
Arguments:
- factors: bfloat16 [96, 256, 1024], P('col'), may hold values from -0.796875 to 0.796875
- metric_root: bfloat16 [1024, 1024], P('row'), may hold values from -1 to 2, as said below
- occ_energy: float32 [96], replicated, may hold values from -3 to -0.5
- vir_energy: float32 [256], replicated, may hold values from 0.2 to 4
- orbital_slot: int32 [96], replicated, may hold values from 0 to 95, each once
- source_plan: int32 [2, 2, 4], P('row'), may hold values from 0 to 95, as said below
- pair_list: int32 [2, 16, 2, 24], P('row', 'col'), may hold values from -1 to 23, as said below
Outputs:
- gamma_fit: float32 [2, 256, 8, 1024], P('row', 'col')
Inputs may be any that keep to these rules, and one draw needn't show every extreme that they name: `metric_root`: Symmetric. `source_plan`: all entries are distinct orbitals. `pair_list`: each list holds 2 to 24 distinct codes k * 6 + l first and -1 in the remaining entries; in every draw some list is full.
All inputs are finite; a program needn't handle non-finite values.
Results may differ from a plain program's by a relative error of at most 0.003.
Values may be sent and summed in bfloat16 or wider, within the bound.
A program may use at most 128 MiB of HBM per device.

v0:
```python
from functools import partial
import jax
import jax.numpy as jnp
from jax import lax
from jax.sharding import PartitionSpec as P


def from_root(shard, axis, root):
    mine = lax.axis_index(axis) == root
    return lax.psum(jnp.where(mine, shard, jnp.zeros_like(shard)), axis)


def fetch_factor(factors, slot_index, owned_slots):
    holder = slot_index // owned_slots
    position = slot_index % owned_slots
    portion = lax.dynamic_index_in_dim(factors, position, 0, keepdims=False)
    return from_root(portion, "col", holder)


def masked_weights(sources, factors, source_energy, local_energy, vir_energy, pair_mask):
    integrals = jnp.einsum("kaq,lbq->klab", sources, factors, preferred_element_type=jnp.float32)
    denominator = (
        source_energy[:, None, None, None]
        + local_energy[None, :, None, None]
        - vir_energy[None, None, :, None]
        - vir_energy[None, None, None, :]
    )
    amplitude = integrals / denominator
    return ((2.0 * amplitude - jnp.swapaxes(amplitude, 2, 3)) * pair_mask[:, :, None, None]).astype(
        jnp.bfloat16
    )


def contract_rows(weights, factors, offset, length):
    return jnp.einsum("klab,lbq->akq", weights, factors, preferred_element_type=jnp.float32)


def fold_metric(flat_gamma, portion):
    return jnp.dot(flat_gamma, portion, preferred_element_type=jnp.float32)


def on_device(factors, metric_root, occ_energy, vir_energy, orbital_slot, source_plan, pair_list):
    owned_slots = factors.shape[0]
    virtual = factors.shape[1]
    aux_count = factors.shape[2]
    columns = lax.axis_size("col")
    steps_count = source_plan.shape[1]
    sources_count = source_plan.shape[2]
    occupied = occ_energy.shape[0]
    column = lax.axis_index("col")
    local_slots = column * owned_slots + jnp.arange(owned_slots, dtype=jnp.int32)
    local_match = orbital_slot[None, :] == local_slots[:, None]
    local_energy = jnp.sum(jnp.where(local_match, occ_energy[None, :], 0.0), axis=1)
    source_match = (
        source_plan[0][:, :, None] == jnp.arange(occupied, dtype=jnp.int32)[None, None, :]
    )
    source_energy = jnp.sum(jnp.where(source_match, occ_energy[None, None, :], 0.0), axis=2)
    source_slot = jnp.sum(jnp.where(source_match, orbital_slot[None, None, :], 0), axis=2)
    code_range = jnp.arange(sources_count * owned_slots, dtype=jnp.int32)
    share_rows = virtual // columns
    makers = []
    for s in range(steps_count):
        sources = jnp.stack(
            [fetch_factor(factors, source_slot[s, k], owned_slots) for k in range(sources_count)]
        )
        code_list = pair_list[0, 0, s]
        pair_mask = (
            jnp.any(code_list[:, None] == code_range[None, :], axis=0)
            .reshape(sources_count, owned_slots)
            .astype(jnp.float32)
        )
        weights = masked_weights(
            sources, factors, source_energy[s], local_energy, vir_energy, pair_mask
        )
        term = partial(contract_rows, weights, factors)
        makers.append(term)
    offset = jnp.int32(0)
    gamma_rows = lax.psum_scatter(
        jnp.concatenate(
            [maker(offset, share_rows * lax.axis_size("col")) for maker in makers], axis=1
        ),
        "col",
        scatter_dimension=0,
        tiled=True,
    )
    flat_gamma = gamma_rows.astype(jnp.bfloat16).reshape(
        share_rows * steps_count * sources_count, aux_count
    )
    fitted = fold_metric(flat_gamma, lax.all_gather(metric_root, "row", axis=0, tiled=True))
    return fitted.reshape(1, share_rows, steps_count * sources_count, aux_count)


def solution(mesh):
    in_specs = (
        P("col", None, None),
        P("row", None),
        P(),
        P(),
        P(),
        P("row", None, None),
        P("row", "col", None, None),
    )
    out_specs = P("row", "col", None, None)
    return jax.shard_map(
        on_device, mesh=mesh, in_specs=in_specs, out_specs=out_specs, check_vma=False
    )
```

profile of v0, /device:TPU:0, one launch (start us, length us, event | category | flops | bytes accessed | tf_op | source)
XLA Modules:
  0.0 309.9 jit_solution(2107653622613330632)
XLA Ops:
  7.4 0.9 select_reduce_fusion.2
  8.3 0.7 fusion.42
  24.3 4.4 %dynamic-slice_select_fusion.7 = (bf16[1,256,1024]{2,1,0:T(8,128)(2,1)}, bf16[1,256,1024]{2,1,0:T(8,128)(2,1)}, bf16[1,256,1024]{2,1,0:T(8,128)(2,1)}, bf16[1,25...) fusion(bf16[6,256,1024]{2,1,0:T(8,128)(2,1)} %param.7, ...), kind=kLoop, calls=%fused_computation.47 | loop fusion | flops 2097152 | bytes 8388648 | tf_op jit(solution)/shard_map/jit(_where)/select_n | solution.py:10
  28.8 0.0 all-gather.2.cloned.1.call-start
  28.8 0.5 all-gather.2.cloned.1.call-update
  29.4 0.2 select_reduce_fusion.1
  29.6 0.2 select_reduce_fusion
  29.8 0.1 fusion.36
  29.9 0.1 reshape.200
  30.0 0.1 reshape.201
  30.1 0.1 broadcast_add_fusion.1
  30.2 0.1 broadcast_subtract_fusion.1
  30.2 113.7 %all-reduce.3.cloned.1.call-done = (bf16[1,256,1024]{2,1,0:T(8,128)(2,1)}, bf16[1,256,1024]{2,1,0:T(8,128)(2,1)}, bf16[1,256,1024]{2,1,0:T(8,128)(2,1)}, bf16[1,...) async-done(((bf16[1,256,1024]{2,1,0:T(8,128)(2,1)}, ...) | async-done | bytes 4194320 | tf_op jit(solution)/shard_map/psum | solution.py:10
  143.9 6.8 %fusion.14 = f32[4,256,6,256]{3,1,2,0:T(8,128)} fusion(bf16[6,256,1024]{2,1,0:T(8,128)(2,1)S(1)} %copy-done.1, bf16[1,256,1024]{2,1,0:T(8,128)(2,1)} %get-tuple-element.9, bf16[1,256,1024]{2,1,0:T(8,128)(2,1)} %get-tuple-element.10, bf16[1,256,1024]{2,1,0:T(8,128)(2,1)} %get-tuple-element.11, bf16[1,256,1024]{2,1,0:T(8,128)(2,1)} %get-tuple-element.12), kind=kOutput, calls=%fused_computation.21 | convolution fusion | flops 3229614080 | bytes 11534336 | tf_op jit(solution)/shard_map/kaq,lbq->klab/dot_general | solution.py:21
  150.8 6.5 %copy.10 = f32[4,256,6,256]{1,3,2,0:T(8,128)} copy(f32[4,256,6,256]{3,1,2,0:T(8,128)} %fusion.14) | data formatting | bytes 12582912 | tf_op jit(solution)/shard_map/kaq,lbq->klab/dot_general | solution.py:21
  157.3 7.2 %fusion.12 = f32[4,256,1024,1]{2,1,3,0:T(8,128)S(1)} fusion(bf16[6,256,1024]{2,1,0:T(8,128)(2,1)S(1)} %copy-done.1, f32[4,256,6,256]{3,1,2,0:T(8,128)} %fusion.14, f32[4,256,6,256]{1,3,2,0:T(8,128)} %copy.10, f32[4,6]{1,0:T(4,128)S(1)} %reshape.200, f32[256]{0:T(256)S(1)} %copy-done.5, f32[4,6,256]{2,1,0:T(8,128)S(1)} %get-tuple-element.21), kind=kOutput, calls=%fused_computation.19 | convolution fusion | flops 3233808384 | bytes 19948640 | tf_op jit(solution)/shard_map/klab,lbq->akq/dot_general | solution.py:35
  164.6 4.6 %copy.19 = f32[4,256,1024,1]{2,0,1,3:T(4,128)} copy(f32[4,256,1024,1]{2,1,3,0:T(8,128)S(1)} %fusion.12) | data formatting | bytes 8388608 | tf_op jit(solution)/shard_map/klab,lbq->akq/dot_general | solution.py:35
  169.2 5.3 %fusion.10 = f32[4,256,6,256]{3,1,2,0:T(8,128)} fusion(bf16[6,256,1024]{2,1,0:T(8,128)(2,1)S(1)} %copy-done.1, bf16[1,256,1024]{2,1,0:T(8,128)(2,1)S(1)} %copy-done.7, bf16[1,256,1024]{2,1,0:T(8,128)(2,1)S(1)} %copy-done.8, bf16[1,256,1024]{2,1,0:T(8,128)(2,1)S(1)} %copy-done.9, bf16[1,256,1024]{2,1,0:T(8,128)(2,1)S(1)} %copy-done.10), kind=kOutput, calls=%fused_computation.17 | convolution fusion | flops 3229614080 | bytes 11534336 | tf_op jit(solution)/shard_map/kaq,lbq->klab/dot_general | solution.py:21
  174.6 6.5 %copy.11 = f32[4,256,6,256]{1,3,2,0:T(8,128)} copy(f32[4,256,6,256]{3,1,2,0:T(8,128)} %fusion.10) | data formatting | bytes 12582912 | tf_op jit(solution)/shard_map/kaq,lbq->klab/dot_general | solution.py:21
  181.1 7.4 %fusion.8 = f32[4,256,1024,1]{2,1,3,0:T(8,128)S(1)} fusion(bf16[6,256,1024]{2,1,0:T(8,128)(2,1)S(1)} %copy-done.1, f32[4,256,6,256]{3,1,2,0:T(8,128)} %fusion.10, f32[4,256,6,256]{1,3,2,0:T(8,128)} %copy.11, f32[4,6]{1,0:T(4,128)S(1)} %reshape.201, f32[4,6,256]{2,1,0:T(8,128)S(1)} %get-tuple-element.22, f32[256]{0:T(256)S(1)} %copy-done.5), kind=kOutput, calls=%fused_computation.15 | convolution fusion | flops 3233808384 | bytes 19948640 | tf_op jit(solution)/shard_map/klab,lbq->akq/dot_general | solution.py:35
  188.5 2.7 copy.18
  191.2 5.4 %pad_maximum_fusion = f32[256,8,1024]{2,1,0:T(8,128)} fusion(f32[256,4,1024]{2,1,0:T(4,128)S(1)} %bitcast.102, f32[256,4,1024]{2,1,0:T(4,128)S(1)} %bitcast.101), kind=kLoop, calls=%fused_computation | loop fusion | flops 2097152 | bytes 16777216 | tf_op jit(solution)/shard_map/concatenate | solution.py:79
  196.7 102.8 %reduce-scatter.2.cloned.1.call-done = f32[16,8,1024]{2,1,0:T(8,128)} async-done(((f32[256,8,1024]{2,1,0:T(8,128)}), f32[16,8,1024]{2,1,0:T(8,128)}) %reduce-scatter.2.cloned.1.call-update) | async-done | bytes 524304 | tf_op jit(solution)/shard_map/reduce_scatter | solution.py:78
  299.5 3.0 fusion.32
  (32 shorter events, 0.2 us)
Async XLA Ops:
  7.4 136.5 %all-reduce.3.cloned.1.call-start = ((), (), s32[]{:S(2)}) async-start(), calls=%async_computation.3 | async-start | bytes 8388608 | tf_op jit(solution)/shard_map/psum | solution.py:10
  28.7 0.7 copy-start.2
  28.7 0.7 copy-start.4
  28.7 0.9 copy-start.3
  28.7 1.1 copy-start.6
  28.7 1.4 copy-start.5
  28.7 115.2 %copy-start.1 = (bf16[6,256,1024]{2,1,0:T(8,128)(2,1)S(1)}, bf16[6,256,1024]{2,1,0:T(8,128)(2,1)}, u32[]{:S(2)}) copy-start(bf16[6,256,1024]{2,1,0:T(8,128)(2,1)} %param.7) | copy-start | bytes 9437188
  28.8 167.9 %all-gather.2.cloned.1.call-start = ((), (), s32[]{:S(2)}) async-start(), calls=%async_computation.2 | async-start | bytes 3145728 | tf_op jit(solution)/shard_map/all_gather | solution.py:89
  29.4 270.1 %reduce-scatter.2.cloned.1.call-start = ((), (), s32[]{:S(2)}) async-start(), calls=%async_computation.1 | async-start | bytes 8912896 | tf_op jit(solution)/shard_map/reduce_scatter | solution.py:78
  164.5 4.7 %copy-start.7 = (bf16[1,256,1024]{2,1,0:T(8,128)(2,1)S(1)}, bf16[1,256,1024]{2,1,0:T(8,128)(2,1)}, u32[]{:S(2)}) copy-start(bf16[1,256,1024]{2,1,0:T(8,128)(2,1)} %get-tuple-element.5) | copy-start | bytes 1572868
  164.5 4.7 %copy-start.8 = (bf16[1,256,1024]{2,1,0:T(8,128)(2,1)S(1)}, bf16[1,256,1024]{2,1,0:T(8,128)(2,1)}, u32[]{:S(2)}) copy-start(bf16[1,256,1024]{2,1,0:T(8,128)(2,1)} %get-tuple-element.6) | copy-start | bytes 1572868
  164.5 4.7 %copy-start.9 = (bf16[1,256,1024]{2,1,0:T(8,128)(2,1)S(1)}, bf16[1,256,1024]{2,1,0:T(8,128)(2,1)}, u32[]{:S(2)}) copy-start(bf16[1,256,1024]{2,1,0:T(8,128)(2,1)} %get-tuple-element.7) | copy-start | bytes 1572868
  164.6 4.7 %copy-start.10 = (bf16[1,256,1024]{2,1,0:T(8,128)(2,1)S(1)}, bf16[1,256,1024]{2,1,0:T(8,128)(2,1)}, u32[]{:S(2)}) copy-start(bf16[1,256,1024]{2,1,0:T(8,128)(2,1)} %get-tuple-element.8) | copy-start | bytes 1572868
  188.5 2.7 copy-start
Sparse Core Ops, SparseCore 0:
  28.9 114.9 all-reduce.2
  196.7 102.7 reduce-scatter.1
Sparse Core Ops, SparseCore 1:
  30.8 35.8 all-gather.1
where the time goes:
time: 310 us
  waiting for transfers between devices  217 us (70%)
  between operations  30.4 us (10%)
  matrix products  29.8 us (10%)
  local copies, waits for them, and re-layouts  21.3 us (7%)
  other arithmetic  11.2 us (4%)
    psum x1, waiting for transfers between devices, from_root(): return lax.psum(jnp.where(mine, shard, jnp.zeros_like(shard)), axis)  114 us
    reduce_scatter x1, waiting for transfers between devices, on_device(): lax.psum_scatter(jnp.concatenate([maker(offset, share_rows * lax.axis_siz...  103 us
    dot_general x2, matrix products, contract_rows(): jnp.einsum('klab,lbq->akq', weights, factors, preferred_element_type=jnp....  14.6 us
    dot_general x2, local copies, waits for them, and re-layouts, masked_weights(): jnp.einsum('kaq,lbq->klab', sources, factors, preferred_element_type=jnp....  13.1 us
    dot_general x2, matrix products, masked_weights(): jnp.einsum('kaq,lbq->klab', sources, factors, preferred_element_type=jnp....  12.2 us
    dot_general x2, local copies, waits for them, and re-layouts, contract_rows(): jnp.einsum('klab,lbq->akq', weights, factors, preferred_element_type=jnp....  7.33 us
  transfers between devices with their start and end apart: 3, of which 2 were waited for; matrix products, arithmetic and copies ran while one was open for 17% of the time, Pallas kernels for 0%

commit v1 on v0

--- a/solution.py
+++ b/solution.py
@@ -5,9 +5,15 @@
 from jax.sharding import PartitionSpec as P
 
 
+def gather_and_add(x, mesh_axis):
+    blocks = lax.all_gather(x, mesh_axis, axis=0, tiled=False)
+    total = blocks.sum(axis=0)
+    return total
+
+
 def from_root(shard, axis, root):
     mine = lax.axis_index(axis) == root
-    return lax.psum(jnp.where(mine, shard, jnp.zeros_like(shard)), axis)
+    return gather_and_add(jnp.where(mine, shard, jnp.zeros_like(shard)), axis)
 
 
 def fetch_factor(factors, slot_index, owned_slots):

time: 310 us -> 787 us (2.54)
  waiting for transfers between devices: 217 us -> 645 us
  other arithmetic: 11.2 us -> 64.4 us
    all_gather x0 -> x8, waiting for transfers between devices: none -> 539 us  [gather_and_add(): blocks = lax.all_gather(x, mesh_axis, axis=0, tiled=False)]
    psum x1 -> x0, waiting for transfers between devices: 114 us -> none  [from_root(): return lax.psum(jnp.where(mine, shard, jnp.zeros_like(shard)), axis)]
    reduce_sum x0 -> x8, other arithmetic: none -> 50.8 us  [gather_and_add(): total = blocks.sum(axis=0)]
  transfers between devices with their start and end apart: 3 -> 10, of which waited for: 2 -> 9; matrix products, arithmetic and copies ran while one was open for 17% -> 8% of each run, Pallas kernels for 0% -> 0%
where the time goes in v1:
time: 787 us; the launch traced here: 786 us
  waiting for transfers between devices  645 us (82%)
  other arithmetic  64.4 us (8%)
  matrix products  30.9 us (4%)
  between operations  29.9 us (4%)
  local copies, waits for them, and re-layouts  15.4 us (2%)
    all_gather x8, waiting for transfers between devices, gather_and_add(): blocks = lax.all_gather(x, mesh_axis, axis=0, tiled=False)  539 us
    reduce_scatter x1, waiting for transfers between devices, on_device(): lax.psum_scatter(jnp.concatenate([maker(offset, share_rows * lax.axis_siz...  102 us
    reduce_sum x8, other arithmetic, gather_and_add(): total = blocks.sum(axis=0)  50.8 us
  transfers between devices with their start and end apart: 10, of which 9 were waited for; matrix products, arithmetic and copies ran while one was open for 8% of the time, Pallas kernels for 0%

profile of v1, /device:TPU:0, one launch (start us, length us, event | category | flops | bytes accessed | tf_op | source)
XLA Modules:
  0.0 786.0 jit_solution(7976282774788656159)
XLA Ops:
  34.1 71.5 %all-gather.14.cloned.1.call-done = bf16[16,256,1024]{2,1,0:T(8,128)(2,1)} async-done(((bf16[1,256,1024]{2,1,0:T(8,128)(2,1)}), bf16[16,256,1024]{2,1,0:T(8,128)(2,1)}) %all-gather.14.cloned.1.call-update) | async-done | bytes 8388624 | tf_op jit(solution)/shard_map/all_gather | solution.py:9
  105.6 6.3 reduce_sum.126
  112.0 68.7 %all-gather.16.cloned.1.call-done = bf16[16,256,1024]{2,1,0:T(8,128)(2,1)} async-done(((bf16[1,256,1024]{2,1,0:T(8,128)(2,1)}), bf16[16,256,1024]{2,1,0:T(8,128)(2,1)}) %all-gather.16.cloned.1.call-update) | async-done | bytes 8388624 | tf_op jit(solution)/shard_map/all_gather | solution.py:9
  180.7 6.3 reduce_sum.127
  187.1 68.7 %all-gather.10.cloned.1.call-done = bf16[16,256,1024]{2,1,0:T(8,128)(2,1)} async-done(((bf16[1,256,1024]{2,1,0:T(8,128)(2,1)}), bf16[16,256,1024]{2,1,0:T(8,128)(2,1)}) %all-gather.10.cloned.1.call-update) | async-done | bytes 8388624 | tf_op jit(solution)/shard_map/all_gather | solution.py:9
  255.8 6.3 reduce_sum.124
  262.1 68.6 %all-gather.12.cloned.1.call-done = bf16[16,256,1024]{2,1,0:T(8,128)(2,1)} async-done(((bf16[1,256,1024]{2,1,0:T(8,128)(2,1)}), bf16[16,256,1024]{2,1,0:T(8,128)(2,1)}) %all-gather.12.cloned.1.call-update) | async-done | bytes 8388624 | tf_op jit(solution)/shard_map/all_gather | solution.py:9
  330.7 6.3 reduce_sum.125
  337.1 6.9 fusion.14
  344.0 6.6 copy.12
  350.6 55.1 %all-gather.18.cloned.1.call-done = bf16[16,256,1024]{2,1,0:T(8,128)(2,1)} async-done(((bf16[1,256,1024]{2,1,0:T(8,128)(2,1)}), bf16[16,256,1024]{2,1,0:T(8,128)(2,1)}) %all-gather.18.cloned.1.call-update) | async-done | bytes 8388624 | tf_op jit(solution)/shard_map/all_gather | solution.py:9
  405.6 6.3 reduce_sum.130
  412.0 68.6 %all-gather.20.cloned.1.call-done = bf16[16,256,1024]{2,1,0:T(8,128)(2,1)} async-done(((bf16[1,256,1024]{2,1,0:T(8,128)(2,1)}), bf16[16,256,1024]{2,1,0:T(8,128)(2,1)}) %all-gather.20.cloned.1.call-update) | async-done | bytes 8388624 | tf_op jit(solution)/shard_map/all_gather | solution.py:9
  480.6 6.4 reduce_sum.131
  487.0 68.7 %all-gather.22.cloned.1.call-done = bf16[16,256,1024]{2,1,0:T(8,128)(2,1)} async-done(((bf16[1,256,1024]{2,1,0:T(8,128)(2,1)}), bf16[16,256,1024]{2,1,0:T(8,128)(2,1)}) %all-gather.22.cloned.1.call-update) | async-done | bytes 8388624 | tf_op jit(solution)/shard_map/all_gather | solution.py:9
  555.6 6.4 reduce_sum.132
  562.0 68.7 %all-gather.24.cloned.1.call-done = bf16[16,256,1024]{2,1,0:T(8,128)(2,1)} async-done(((bf16[1,256,1024]{2,1,0:T(8,128)(2,1)}), bf16[16,256,1024]{2,1,0:T(8,128)(2,1)}) %all-gather.24.cloned.1.call-update) | async-done | bytes 8388624 | tf_op jit(solution)/shard_map/all_gather | solution.py:9
  630.7 6.3 reduce_sum.133
  637.1 6.8 fusion.10
  643.9 6.7 copy.14
  650.6 8.2 %fusion.18 = f32[256,4,1024]{2,0,1:T(8,128)S(1)} fusion(bf16[6,256,1024]{2,1,0:T(8,128)(2,1)} %param.7, f32[4,256,6,256]{3,1,2,0:T(8,128)} %fusion.14, f32[4,256,6,256]{1,3,2,0:T(8,128)} %copy.12, f32[4,6]{1,0:T(4,128)S(1)} %reshape.168, f32[256]{0:T(256)S(1)} %copy-done.6, f32[4,6,256]{2,1,0:T(8,128)S(1)} %get-tuple-element.13), kind=kOutput, calls=%fused_computation.21 | convolution fusion | flops 3233808384 | bytes 19948640 | tf_op jit(solution)/shard_map/klab,lbq->akq/dot_general | solution.py:41
  660.1 5.9 fusion.23
  666.0 6.7 pad_maximum_fusion
  673.3 101.5 %reduce-scatter.2.cloned.1.call-done = f32[16,8,1024]{2,0,1:T(8,128)} async-done(((f32[256,8,1024]{2,0,1:T(8,128)}), f32[16,8,1024]{2,0,1:T(8,128)}) %reduce-scatter.2.cloned.1.call-update) | async-done | bytes 524304 | tf_op jit(solution)/shard_map/reduce_scatter | solution.py:84
  (59 shorter events, 17.2 us)
Async XLA Ops:
  7.4 98.3 %all-gather.14.cloned.1.call-start = ((), (), s32[]{:S(2)}) async-start(), calls=%async_computation.3 | async-start | bytes 8912896 | tf_op jit(solution)/shard_map/all_gather | solution.py:9
  28.5 4.8 copy-start.7
  28.5 5.1 copy-start.3
  28.5 5.1 copy-start.5
  28.5 5.3 copy-start.4
  28.5 5.5 copy-start.6
  28.5 152.2 %all-gather.16.cloned.1.call-start = ((), (), s32[]{:S(2)}) async-start(), calls=%async_computation.4 | async-start | bytes 8912896 | tf_op jit(solution)/shard_map/all_gather | solution.py:9
  29.3 226.5 %all-gather.10.cloned.1.call-start = ((), (), s32[]{:S(2)}) async-start(), calls=%async_computation.1 | async-start | bytes 8912896 | tf_op jit(solution)/shard_map/all_gather | solution.py:9
  30.0 300.7 %all-gather.12.cloned.1.call-start = ((), (), s32[]{:S(2)}) async-start(), calls=%async_computation.2 | async-start | bytes 8912896 | tf_op jit(solution)/shard_map/all_gather | solution.py:9
  30.6 375.1 %all-gather.18.cloned.1.call-start = ((), (), s32[]{:S(2)}) async-start(), calls=%async_computation.5 | async-start | bytes 8912896 | tf_op jit(solution)/shard_map/all_gather | solution.py:9
  31.2 449.4 %all-gather.20.cloned.1.call-start = ((), (), s32[]{:S(2)}) async-start(), calls=%async_computation.6 | async-start | bytes 8912896 | tf_op jit(solution)/shard_map/all_gather | solution.py:9
  31.7 523.9 %all-gather.22.cloned.1.call-start = ((), (), s32[]{:S(2)}) async-start(), calls=%async_computation.7 | async-start | bytes 8912896 | tf_op jit(solution)/shard_map/all_gather | solution.py:9
  32.5 598.2 %all-gather.24.cloned.1.call-start = ((), (), s32[]{:S(2)}) async-start(), calls=%async_computation.8 | async-start | bytes 8912896 | tf_op jit(solution)/shard_map/all_gather | solution.py:9
  33.2 741.6 %reduce-scatter.2.cloned.1.call-start = ((), (), s32[]{:S(2)}) async-start(), calls=%async_computation.9 | async-start | bytes 8912896 | tf_op jit(solution)/shard_map/reduce_scatter | solution.py:84
  262.1 74.9 %copy-start.1 = (bf16[6,256,1024]{2,1,0:T(8,128)(2,1)S(1)}, bf16[6,256,1024]{2,1,0:T(8,128)(2,1)}, u32[]{:S(2)}) copy-start(bf16[6,256,1024]{2,1,0:T(8,128)(2,1)} %param.7) | copy-start | bytes 9437188
  643.9 15.0 %slice-start = ((s8[6291456]{0:T(1024)(128)(4,1)}), s8[2097152]{0:T(1024)(128)(4,1)S(1)}, s32[]{:S(2)}) async-start(s8[6291456]{0:T(1024)(128)(4,1)} %bitcast.121), calls=%async_computation.11 | async-start | bytes 4194304
  650.6 8.3 %slice-start.1 = ((s8[6291456]{0:T(1024)(128)(4,1)}), s8[4194304]{0:T(1024)(128)(4,1)S(1)}, s32[]{:S(2)}) async-start(s8[6291456]{0:T(1024)(128)(4,1)} %bitcast.121), calls=%async_computation.12 | async-start | bytes 8388608
  650.6 8.6 %copy-start = (f32[4,256,6,256]{1,3,2,0:T(8,128)S(1)}, f32[4,256,6,256]{1,3,2,0:T(8,128)}, u32[]{:S(2)}) copy-start(f32[4,256,6,256]{1,3,2,0:T(8,128)} %copy.14) | copy-start | bytes 18874372
  650.6 9.5 %copy-start.2 = (bf16[6,256,1024]{2,1,0:T(8,128)(2,1)S(1)}, bf16[6,256,1024]{2,1,0:T(8,128)(2,1)}, u32[]{:S(2)}) copy-start(bf16[6,256,1024]{2,1,0:T(8,128)(2,1)} %param.7) | copy-start | bytes 9437188
  672.7 103.2 %all-gather.26.cloned.1.call-start = ((), (), s32[]{:S(2)}) async-start(), calls=%async_computation.10 | async-start | bytes 3145728 | tf_op jit(solution)/shard_map/all_gather | solution.py:95
Sparse Core Ops, SparseCore 0:
  28.6 76.9 all-gather.13
  107.8 72.8 all-gather.15
  182.9 72.8 all-gather.9
  257.8 72.8 all-gather.11
  332.7 72.8 all-gather.17
  407.7 72.8 all-gather.19
  482.7 72.8 all-gather.21
  557.8 72.8 all-gather.23
  672.8 101.9 reduce-scatter.1
Sparse Core Ops, SparseCore 1:
  674.7 31.5 all-gather.25
